TPU v7x, 32 devices: a whole 2x2x4 slice. The times are simulated.
32 devices in a mesh: depth: 16 (over z, x, core), band: 2 (over y).
Axes of the slice: x: 2, y: 2, z: 4, core: 2. Of those that a mesh axis runs over, the one named last changes fastest.
Arguments:
- volume: int32 [64, 64, 1024], P('depth', 'band'), may hold values from 0 to 255
- tf_table: int32 [4, 256], replicated, may hold values from 0 to 255
- view_code: int32 [2, 4], replicated, may hold values from -20 to 20
Outputs:
- final_image: float32 [2, 1024, 4, 64], P(None, 'depth', None, 'band')
All inputs are finite; a program needn't handle non-finite values.
Results may differ from a plain program's by a relative error of at most 0.0014.
Values may be sent and summed in bfloat16 or wider, within the bound.
A program may use at most 64 MiB of HBM per device.

v0:
```python
import math

import jax
import jax.numpy as jnp
from jax import lax
from jax.sharding import PartitionSpec as P

VIEWS = 2
MARGIN = 16


def extended(x, sides, width):
    for axis, dim in sides:
        size, length = (lax.axis_size(axis), x.shape[dim])
        up = [(i, (i + 1) % size) for i in range(size - 1)]
        down = [(j, i) for i, j in up]
        last = lax.slice_in_dim(x, length - width, length, axis=dim)
        first = lax.slice_in_dim(x, 0, width, axis=dim)
        before = lax.ppermute(last, axis, up)
        after = lax.ppermute(first, axis, down)
        x = jnp.concatenate([before, x, after], axis=dim)
    return x


def lanczos(offset):
    return jnp.where(jnp.abs(offset) < 3.0, jnp.sinc(offset) * jnp.sinc(offset / 3.0), 0.0)


def split_offset(coefficient, position, length, lift=0):
    numerator = coefficient * (2 * position + 1 - length) + lift * length
    integer_part = numerator // (2 * length)
    fraction = (numerator - integer_part * (2 * length)).astype(jnp.float32) / (2.0 * length)
    return (integer_part, fraction)


def make_palette(tf_table, depth_count):
    table_float = tf_table.astype(jnp.float32)
    opacity = table_float[3] / (64.0 * depth_count)
    premult = table_float[0:3] / 255.0 * opacity
    return jnp.concatenate([premult, opacity[None]], axis=0).astype(jnp.bfloat16)


def classify(codes, palette):
    shape = codes.shape
    last = shape[-1]
    rows = codes.reshape(-1, last)
    row_count = rows.shape[0]
    group_rows = math.gcd(row_count, 8)
    grouped = rows.reshape(row_count // group_rows, group_rows, last)
    table = palette.reshape(4, 16, 16)
    levels = jnp.arange(16, dtype=jnp.int32)

    def lookup(block_codes):
        high_part = block_codes // 16
        low_part = block_codes - high_part * 16
        low_hot = (low_part[None] == levels[:, None, None]).astype(jnp.bfloat16)
        partial_value = jnp.einsum(
            "chl,lgk->chgk", table, low_hot, preferred_element_type=jnp.float32
        )
        high_hot = (high_part[None] == levels[:, None, None]).astype(jnp.float32)
        return jnp.sum(partial_value * high_hot[None], axis=1)

    picked = lax.map(lookup, grouped)
    picked = jnp.transpose(picked, (1, 0, 2, 3)).reshape((4,) + shape)
    return picked.astype(jnp.bfloat16)


def column_weights(integer_part, fraction, block):
    inputs = jnp.arange(3 * block, dtype=jnp.int32)[:, None]
    outputs = jnp.arange(block, dtype=jnp.int32)[None, :]
    distance = inputs - block - outputs - integer_part
    return lanczos(fraction - distance.astype(jnp.float32)).astype(jnp.bfloat16)


def row_weights(integer_part, fraction, out_rows, in_rows, margin):
    outputs = jnp.arange(out_rows, dtype=jnp.int32)[:, None]
    inputs = jnp.arange(in_rows, dtype=jnp.int32)[None, :]
    distance = inputs - margin - outputs - integer_part
    return lanczos(fraction - distance.astype(jnp.float32)).astype(jnp.bfloat16)


def warp_weights(coefficient, first_column, strip_width, margin, total_width):
    columns = first_column + jnp.arange(strip_width, dtype=jnp.int32)
    integer_part, fraction = split_offset(coefficient, columns, total_width, 1)
    inputs = jnp.arange(strip_width + 2 * margin, dtype=jnp.int32)[None, :]
    outputs = jnp.arange(strip_width, dtype=jnp.int32)[:, None]
    distance = inputs - margin - outputs - integer_part[:, None]
    return lanczos(fraction[:, None] - distance.astype(jnp.float32))


def shear_columns(source, tap_matrix, block):
    channels, row_count, extent = source.shape
    blocks = extent // block
    padded = jnp.pad(source, ((0, 0), (0, 0), (block, block)))
    tile_view = padded.reshape(channels, row_count, blocks + 2, block)
    windows = jnp.concatenate(
        [
            tile_view[:, :, 0:blocks],
            tile_view[:, :, 1 : blocks + 1],
            tile_view[:, :, 2 : blocks + 2],
        ],
        axis=3,
    )
    result = jnp.einsum("crbk,kj->bjcr", windows, tap_matrix, preferred_element_type=jnp.float32)
    return result.reshape(extent, channels, row_count).astype(jnp.bfloat16)


def shear_rows(source, tap_matrix):
    return jnp.einsum("xcr,yr->xcy", source, tap_matrix, preferred_element_type=jnp.float32)


def over(front_part, back_part):
    return front_part + (1.0 - front_part[..., 3:4, :]) * back_part


def body(volume, tf_table, view_code):
    slab_count, band_rows, extent = volume.shape
    depth_size = lax.axis_size("depth")
    depth_rank = lax.axis_index("depth")
    total_depth = slab_count * depth_size
    block = min(128, extent)
    strip_width = extent // depth_size
    widened_rows = band_rows + 2 * MARGIN
    palette = make_palette(tf_table, total_depth)
    classified = classify(volume, palette)
    widened = extended(classified, (("band", 2),), MARGIN)
    finals = []
    for view_index in range(VIEWS):
        params = view_code[view_index]
        facing = params[3] >= 0
        picture = jnp.zeros((extent, 4, band_rows), jnp.float32)
        for step_index in range(slab_count):
            local_slice = jnp.where(facing, step_index, slab_count - 1 - step_index).astype(
                jnp.int32
            )
            global_slice = depth_rank * slab_count + local_slice
            whole_y, frac_y = split_offset(params[1], global_slice, total_depth)
            whole_x, frac_x = split_offset(params[0], global_slice, total_depth)
            current = lax.dynamic_index_in_dim(widened, local_slice, 1, keepdims=False)
            row_sheared = shear_columns(current, column_weights(whole_x, frac_x, block), block)
            sheared = shear_rows(
                row_sheared, row_weights(whole_y, frac_y, band_rows, widened_rows, MARGIN)
            )
            picture = over(picture, sheared)
        pieces = picture.reshape(depth_size, strip_width, 4, band_rows)
        arrived = lax.all_to_all(
            pieces.astype(jnp.bfloat16), "depth", split_axis=0, concat_axis=0, tiled=True
        ).astype(pieces.dtype)
        for level_index in range(depth_size.bit_length() - 1):
            paired = arrived.reshape((arrived.shape[0] // 2, 2) + arrived.shape[1:])
            earlier = paired[:, 0]
            later = paired[:, 1]
            front_part = jnp.where(facing, earlier, later)
            back_part = jnp.where(facing, later, earlier)
            arrived = over(front_part, back_part)
        strip = arrived[0]
        padded_strip = extended(strip, (("depth", 0),), MARGIN)
        weights = warp_weights(params[2], depth_rank * strip_width, strip_width, MARGIN, extent)
        final_strip = jnp.einsum(
            "ck,kay->cay",
            weights,
            padded_strip,
            precision=lax.Precision.HIGHEST,
            preferred_element_type=jnp.float32,
        )
        finals.append(final_strip)
    return jnp.stack(finals)


def solution(mesh):
    placed = (P("depth", "band", None), P(), P())
    return jax.shard_map(
        body, mesh=mesh, in_specs=placed, out_specs=P(None, "depth", None, "band"), check_vma=False
    )
```

profile of v0, /device:TPU:8, one launch (start us, length us, event | category | flops | bytes accessed | tf_op | source)
XLA Modules:
  0.0 122.0 jit_solution(5489275752223972056)
XLA Ops:
  0.9 24.4 %while.14 = (s32[]{:T(128)}, bf16[16,4,8,1024]{3,2,0,1:T(8,128)(2,1)S(1)}, s32[16,8,1024]{2,1,0:T(8,128)}, bf16[4,16,16]{2,1,0:T(8,128)(2,1)S(1)}, s32[]{:T(128)}) while((s32[]{:T(128)}, bf16[16,4,8,1024]{3,2,0,1:T(8,128)(2,1)S(1)}, s32[16,8,1024]{2,1,0:T(8,128)}, bf16[4,16,16]{2,1,0:T(8,128)(2,1)S(1)}, s32[]{:T(128)}) %tuple.78), condition=%wide.region_2.5_spmd.clone.clone, body=%wide.region_0.4_spmd.clone.clone.sunk | while | flops 18325504 | bytes 1411149 | solution.py:63
  0.9 0.8 subtract_bitcast_fusion.2
  2.5 0.8 subtract_bitcast_fusion.2
  4.0 0.8 subtract_bitcast_fusion.2
  5.5 0.8 subtract_bitcast_fusion.2
  7.0 0.8 subtract_bitcast_fusion.2
  13.1 0.8 subtract_bitcast_fusion.2
  16.2 0.8 subtract_bitcast_fusion.2
  17.7 0.8 subtract_bitcast_fusion.2
  19.2 0.8 subtract_bitcast_fusion.2
  25.5 1.3 %collective-permute-start.1 = (bf16[4,4,16,1024]{3,2,1,0:T(8,128)(2,1)S(1)}, bf16[4,4,16,1024]{3,2,1,0:T(8,128)(2,1)S(1)}, u32[]{:S(2)}, u32[]{:S(2)}) collective-permute-start(bf16[4,4,16,1024]{3,2,1,0:T(8,128)(2,1)S(1)} %get-tuple-element.149), channel_id=1, source_target_pairs={{1,0},{3,2},{5,4},{7,6},{9,8},{11,10},{13,12},{15,14},{17,16},{19,... | collective-permute-start | bytes 1572872 | tf_op jit(solution)/shard_map/ppermute | solution.py:20
  26.8 4.6 %collective-permute-start = (bf16[4,4,16,1024]{3,2,1,0:T(8,128)(2,1)S(1)}, bf16[4,4,16,1024]{3,2,1,0:T(8,128)(2,1)S(1)}, u32[]{:S(2)}, u32[]{:S(2)}) collective-permute-start(bf16[4,4,16,1024]{3,2,1,0:T(8,128)(2,1)S(1)} %get-tuple-element.148), channel_id=1, source_target_pairs={{0,1},{2,3},{4,5},{6,7},{8,9},{10,11},{12,13},{14,15},{16,17},{18,... | collective-permute-start | bytes 1572872 | tf_op jit(solution)/shard_map/ppermute | solution.py:19
  43.9 1.2 and_select_fusion
  45.1 1.2 convert_multiply_fusion
  48.5 1.7 %dynamic-slice_bitcast_fusion.4 = (bf16[4,64,1024]{2,1,0:T(8,128)(2,1)S(1)}, bf16[4,64,1024]{2,1,0:T(8,128)(2,1)}, bf16[4,64,1024]{2,1,0:T(8,128)(2,1)}, bf16[4,...) fusion(bf16[4,4,64,1024]{3,2,1,0:T(8,128)(2,1)S(1)} %pad_maximu, ...), kind=kLoop, calls=%fused_computation.126 | loop fusion | bytes 8388640 | tf_op jit(solution)/shard_map/jit(dynamic_index_in_dim)/squeeze | solution.py:139
  51.1 0.9 copy.254
  52.0 0.9 copy.253
  53.8 0.9 copy.258
  54.7 0.9 copy.257
  55.6 0.9 copy.256
  56.5 1.1 fusion.95
  58.6 0.9 copy.261
  59.6 0.9 copy.260
  60.5 0.9 copy.259
  61.5 1.1 fusion.98
  65.7 1.1 fusion.101
  67.0 1.1 fusion.104
  68.9 1.1 reshape.474
  70.0 6.3 %all-to-all-start.1 = ((bf16[16,2,4096]{2,1,0:T(2,128)(2,1)}), bf16[16,2,4096]{2,1,0:T(2,128)(2,1)S(1)}, u32[]{:S(2)}, u32[]{:S(2)}) async-start(bf16[16,2,4096]{2,1,0:T(2,128)(2,1)} %reshape.474), calls=%async_computation.1 | async-start | bytes 524288 | tf_op jit(solution)/shard_map/all_to_all | solution.py:146
  77.1 0.9 copy.242
  78.1 0.9 copy.241
  79.8 0.9 copy.246
  80.7 0.9 copy.245
  81.6 0.9 copy.244
  82.6 1.1 fusion.83
  85.5 0.9 copy.248
  86.4 0.9 copy.247
  87.3 1.1 fusion.86
  91.3 1.1 fusion.89
  92.4 1.1 fusion.92
  94.5 1.1 reshape.476
  95.6 6.0 %all-to-all-start = ((bf16[16,2,4096]{2,1,0:T(2,128)(2,1)}), bf16[16,2,4096]{2,1,0:T(2,128)(2,1)S(1)}, u32[]{:S(2)}, u32[]{:S(2)}) async-start(bf16[16,2,4096]{2,1,0:T(2,128)(2,1)} %reshape.476), calls=%async_computation | async-start | bytes 524288 | tf_op jit(solution)/shard_map/all_to_all | solution.py:146
  102.7 3.1 %collective-permute-start.5 = (f32[16,4,32]{0,2,1:T(8,128)S(1)}, f32[16,4,32]{0,2,1:T(8,128)S(1)}, u32[]{:S(2)}, u32[]{:S(2)}) collective-permute-start(f32[16,4,32]{0,2,1:T(8,128)S(1)} %get-tuple-element.157), channel_id=1, source_target_pairs={{2,0},{4,2},{6,4},{8,6},{10,8},{12,10},{14,12},{16,14},{18,16},{20... | collective-permute-start | bytes 24584 | tf_op jit(solution)/shard_map/ppermute | solution.py:20
  105.8 1.9 %collective-permute-start.4 = (f32[16,4,32]{0,2,1:T(8,128)S(1)}, f32[16,4,32]{0,2,1:T(8,128)S(1)}, u32[]{:S(2)}, u32[]{:S(2)}) collective-permute-start(f32[16,4,32]{0,2,1:T(8,128)S(1)} %get-tuple-element.156), channel_id=1, source_target_pairs={{0,2},{2,4},{4,6},{6,8},{8,10},{10,12},{12,14},{14,16},{16,18},{18... | collective-permute-start | bytes 24584 | tf_op jit(solution)/shard_map/ppermute | solution.py:19
  107.7 1.5 %all-to-all-done = bf16[16,2,4096]{2,1,0:T(2,128)(2,1)S(1)} async-done(((bf16[16,2,4096]{2,1,0:T(2,128)(2,1)}), bf16[16,2,4096]{2,1,0:T(2,128)(2,1)S(1)}, u32[]{:S(2)}, u32[]{:S(2)}) %all-to-all-start) | async-done | bytes 262176 | tf_op jit(solution)/shard_map/all_to_all | solution.py:146
  110.3 4.0 %collective-permute-start.3 = (f32[16,4,32]{0,2,1:T(8,128)S(1)}, f32[16,4,32]{0,2,1:T(8,128)S(1)}, u32[]{:S(2)}, u32[]{:S(2)}) collective-permute-start(f32[16,4,32]{0,2,1:T(8,128)S(1)} %get-tuple-element.155), channel_id=1, source_target_pairs={{2,0},{4,2},{6,4},{8,6},{10,8},{12,10},{14,12},{16,14},{18,16},{20... | collective-permute-start | bytes 24584 | tf_op jit(solution)/shard_map/ppermute | solution.py:20
  114.3 1.9 %collective-permute-start.2 = (f32[16,4,32]{0,2,1:T(8,128)S(1)}, f32[16,4,32]{0,2,1:T(8,128)S(1)}, u32[]{:S(2)}, u32[]{:S(2)}) collective-permute-start(f32[16,4,32]{0,2,1:T(8,128)S(1)} %get-tuple-element.154), channel_id=1, source_target_pairs={{0,2},{2,4},{4,6},{6,8},{8,10},{10,12},{12,14},{14,16},{16,18},{18... | collective-permute-start | bytes 24584 | tf_op jit(solution)/shard_map/ppermute | solution.py:19
  116.8 4.0 %collective-permute-done.2 = f32[16,4,32]{0,2,1:T(8,128)S(1)} collective-permute-done((f32[16,4,32]{0,2,1:T(8,128)S(1)}, f32[16,4,32]{0,2,1:T(8,128)S(1)}, u32[]{:S(2)}, u32[]{:S(2)}) %collective-permute-start.2) | collective-permute-done | bytes 8224 | tf_op jit(solution)/shard_map/ppermute | solution.py:19
  (217 shorter events, 38.1 us)
Async XLA Ops:
  25.3 6.0 %copy-start.22 = (s32[2,4]{1,0:T(2,128)S(1)}, s32[2,4]{1,0:T(2,128)}, u32[]{:S(2)}) copy-start(s32[2,4]{1,0:T(2,128)} %param.10) | copy-start | bytes 100
  25.5 22.7 %collective-permute-start.1 = (bf16[4,4,16,1024]{3,2,1,0:T(8,128)(2,1)S(1)}, bf16[4,4,16,1024]{3,2,1,0:T(8,128)(2,1)S(1)}, u32[]{:S(2)}, u32[]{:S(2)}) collective-permute-start(bf16[4,4,16,1024]{3,2,1,0:T(8,128)(2,1)S(1)} %get-tuple-element.149), channel_id=1, source_target_pairs={{1,0},{3,2},{5,4},{7,6},{9,8},{11,10},{13,12},{15,14},{17,16},{19,... | collective-permute-start | bytes 1572872 | tf_op jit(solution)/shard_map/ppermute | solution.py:20
  26.8 21.4 %collective-permute-start = (bf16[4,4,16,1024]{3,2,1,0:T(8,128)(2,1)S(1)}, bf16[4,4,16,1024]{3,2,1,0:T(8,128)(2,1)S(1)}, u32[]{:S(2)}, u32[]{:S(2)}) collective-permute-start(bf16[4,4,16,1024]{3,2,1,0:T(8,128)(2,1)S(1)} %get-tuple-element.148), channel_id=1, source_target_pairs={{0,1},{2,3},{4,5},{6,7},{8,9},{10,11},{12,13},{14,15},{16,17},{18,... | collective-permute-start | bytes 1572872 | tf_op jit(solution)/shard_map/ppermute | solution.py:19
  53.7 2.8 %copy-start.16 = (bf16[4,64,8,128]{3,1,2,0:T(8,128)(2,1)S(1)}, bf16[4,64,8,128]{3,1,2,0:T(8,128)(2,1)}, u32[]{:S(2)}) copy-start(bf16[4,64,8,128]{3,1,2,0:T(8,128)(2,1)} %copy.254) | copy-start | bytes 1572868
  53.7 2.8 %copy-start.18 = (bf16[4,64,8,128]{3,1,2,0:T(8,128)(2,1)S(1)}, bf16[4,64,8,128]{3,1,2,0:T(8,128)(2,1)}, u32[]{:S(2)}) copy-start(bf16[4,64,8,128]{3,1,2,0:T(8,128)(2,1)} %copy.253) | copy-start | bytes 1572868
  56.5 1.3 %copy-start.4 = (bf16[4,64,1024]{2,1,0:T(8,128)(2,1)S(1)}, bf16[4,64,1024]{2,1,0:T(8,128)(2,1)}, u32[]{:S(2)}) copy-start(bf16[4,64,1024]{2,1,0:T(8,128)(2,1)} %get-tuple-element.114) | copy-start | bytes 1572868
  58.6 2.8 %copy-start.9 = (bf16[4,64,8,128]{3,1,2,0:T(8,128)(2,1)S(1)}, bf16[4,64,8,128]{3,1,2,0:T(8,128)(2,1)}, u32[]{:S(2)}) copy-start(bf16[4,64,8,128]{3,1,2,0:T(8,128)(2,1)} %copy.258) | copy-start | bytes 1572868
  58.6 2.8 %copy-start.11 = (bf16[4,64,8,128]{3,1,2,0:T(8,128)(2,1)S(1)}, bf16[4,64,8,128]{3,1,2,0:T(8,128)(2,1)}, u32[]{:S(2)}) copy-start(bf16[4,64,8,128]{3,1,2,0:T(8,128)(2,1)} %copy.257) | copy-start | bytes 1572868
  58.6 2.8 %copy-start.14 = (bf16[4,64,8,128]{3,1,2,0:T(8,128)(2,1)S(1)}, bf16[4,64,8,128]{3,1,2,0:T(8,128)(2,1)}, u32[]{:S(2)}) copy-start(bf16[4,64,8,128]{3,1,2,0:T(8,128)(2,1)} %copy.256) | copy-start | bytes 1572868
  62.5 1.0 copy-start.3
  64.3 1.0 copy-start.6
  64.3 1.2 copy-start.7
  64.3 1.3 %copy-start.12 = (bf16[4,64,8,128]{3,1,2,0:T(8,128)(2,1)S(1)}, bf16[4,64,8,128]{3,1,2,0:T(8,128)(2,1)}, u32[]{:S(2)}) copy-start(bf16[4,64,8,128]{3,1,2,0:T(8,128)(2,1)} %copy.259) | copy-start | bytes 1572868
  68.1 8.1 %copy-start.2 = (bf16[4,64,1024]{2,1,0:T(8,128)(2,1)S(1)}, bf16[4,64,1024]{2,1,0:T(8,128)(2,1)}, u32[]{:S(2)}) copy-start(bf16[4,64,1024]{2,1,0:T(8,128)(2,1)} %get-tuple-element.119) | copy-start | bytes 1572868
  70.0 25.6 %all-to-all-start.1 = ((bf16[16,2,4096]{2,1,0:T(2,128)(2,1)}), bf16[16,2,4096]{2,1,0:T(2,128)(2,1)S(1)}, u32[]{:S(2)}, u32[]{:S(2)}) async-start(bf16[16,2,4096]{2,1,0:T(2,128)(2,1)} %reshape.474), calls=%async_computation.1 | async-start | bytes 524288 | tf_op jit(solution)/shard_map/all_to_all | solution.py:146
  77.0 2.0 %copy-start.1 = (bf16[4,64,1024]{2,1,0:T(8,128)(2,1)S(1)}, bf16[4,64,1024]{2,1,0:T(8,128)(2,1)}, u32[]{:S(2)}) copy-start(bf16[4,64,1024]{2,1,0:T(8,128)(2,1)} %get-tuple-element.118) | copy-start | bytes 1572868
  79.7 2.8 %copy-start.17 = (bf16[4,64,8,128]{3,1,2,0:T(8,128)(2,1)S(1)}, bf16[4,64,8,128]{3,1,2,0:T(8,128)(2,1)}, u32[]{:S(2)}) copy-start(bf16[4,64,8,128]{3,1,2,0:T(8,128)(2,1)} %copy.242) | copy-start | bytes 1572868
  79.7 2.8 %copy-start.19 = (bf16[4,64,8,128]{3,1,2,0:T(8,128)(2,1)S(1)}, bf16[4,64,8,128]{3,1,2,0:T(8,128)(2,1)}, u32[]{:S(2)}) copy-start(bf16[4,64,8,128]{3,1,2,0:T(8,128)(2,1)} %copy.241) | copy-start | bytes 1572868
  82.6 2.0 %copy-start = (bf16[4,64,1024]{2,1,0:T(8,128)(2,1)S(1)}, bf16[4,64,1024]{2,1,0:T(8,128)(2,1)}, u32[]{:S(2)}) copy-start(bf16[4,64,1024]{2,1,0:T(8,128)(2,1)} %get-tuple-element.117) | copy-start | bytes 1572868
  85.3 2.0 %copy-start.10 = (bf16[4,64,8,128]{3,1,2,0:T(8,128)(2,1)S(1)}, bf16[4,64,8,128]{3,1,2,0:T(8,128)(2,1)}, u32[]{:S(2)}) copy-start(bf16[4,64,8,128]{3,1,2,0:T(8,128)(2,1)} %copy.246) | copy-start | bytes 1572868
  85.3 2.0 %copy-start.13 = (bf16[4,64,8,128]{3,1,2,0:T(8,128)(2,1)S(1)}, bf16[4,64,8,128]{3,1,2,0:T(8,128)(2,1)}, u32[]{:S(2)}) copy-start(bf16[4,64,8,128]{3,1,2,0:T(8,128)(2,1)} %copy.245) | copy-start | bytes 1572868
  85.3 2.0 %copy-start.15 = (bf16[4,64,8,128]{3,1,2,0:T(8,128)(2,1)S(1)}, bf16[4,64,8,128]{3,1,2,0:T(8,128)(2,1)}, u32[]{:S(2)}) copy-start(bf16[4,64,8,128]{3,1,2,0:T(8,128)(2,1)} %copy.244) | copy-start | bytes 1572868
  87.3 1.1 copy-start.21
  90.1 1.0 copy-start.5
  90.1 1.2 copy-start.8
  92.4 1.1 copy-start.20
  95.6 13.6 %all-to-all-start = ((bf16[16,2,4096]{2,1,0:T(2,128)(2,1)}), bf16[16,2,4096]{2,1,0:T(2,128)(2,1)S(1)}, u32[]{:S(2)}, u32[]{:S(2)}) async-start(bf16[16,2,4096]{2,1,0:T(2,128)(2,1)} %reshape.476), calls=%async_computation | async-start | bytes 524288 | tf_op jit(solution)/shard_map/all_to_all | solution.py:146
  102.7 13.6 %collective-permute-start.5 = (f32[16,4,32]{0,2,1:T(8,128)S(1)}, f32[16,4,32]{0,2,1:T(8,128)S(1)}, u32[]{:S(2)}, u32[]{:S(2)}) collective-permute-start(f32[16,4,32]{0,2,1:T(8,128)S(1)} %get-tuple-element.157), channel_id=1, source_target_pairs={{2,0},{4,2},{6,4},{8,6},{10,8},{12,10},{14,12},{16,14},{18,16},{20... | collective-permute-start | bytes 24584 | tf_op jit(solution)/shard_map/ppermute | solution.py:20
  105.8 10.5 %collective-permute-start.4 = (f32[16,4,32]{0,2,1:T(8,128)S(1)}, f32[16,4,32]{0,2,1:T(8,128)S(1)}, u32[]{:S(2)}, u32[]{:S(2)}) collective-permute-start(f32[16,4,32]{0,2,1:T(8,128)S(1)} %get-tuple-element.156), channel_id=1, source_target_pairs={{0,2},{2,4},{4,6},{6,8},{8,10},{10,12},{12,14},{14,16},{16,18},{18... | collective-permute-start | bytes 24584 | tf_op jit(solution)/shard_map/ppermute | solution.py:19
  109.9 6.5 %copy-start.23 = (s32[64]{0:T(128)S(1)}, s32[64]{0:T(128)}, u32[]{:S(2)}) copy-start(s32[64]{0:T(128)} %and_select_fusion) | copy-start | bytes 772
  109.9 6.5 %copy-start.24 = (f32[64]{0:T(128)S(1)}, f32[64]{0:T(128)}, u32[]{:S(2)}) copy-start(f32[64]{0:T(128)} %convert_multiply_fusion) | copy-start | bytes 772
  109.9 6.5 %copy-start.25 = (s32[96]{0:T(128)S(1)}, s32[96]{0:T(128)}, u32[]{:S(2)}) copy-start(s32[96]{0:T(128)} %iota_add_fusion.2) | copy-start | bytes 1156
  110.3 6.5 %collective-permute-start.3 = (f32[16,4,32]{0,2,1:T(8,128)S(1)}, f32[16,4,32]{0,2,1:T(8,128)S(1)}, u32[]{:S(2)}, u32[]{:S(2)}) collective-permute-start(f32[16,4,32]{0,2,1:T(8,128)S(1)} %get-tuple-element.155), channel_id=1, source_target_pairs={{2,0},{4,2},{6,4},{8,6},{10,8},{12,10},{14,12},{16,14},{18,16},{20... | collective-permute-start | bytes 24584 | tf_op jit(solution)/shard_map/ppermute | solution.py:20
  114.3 6.5 %collective-permute-start.2 = (f32[16,4,32]{0,2,1:T(8,128)S(1)}, f32[16,4,32]{0,2,1:T(8,128)S(1)}, u32[]{:S(2)}, u32[]{:S(2)}) collective-permute-start(f32[16,4,32]{0,2,1:T(8,128)S(1)} %get-tuple-element.154), channel_id=1, source_target_pairs={{0,2},{2,4},{4,6},{6,8},{8,10},{10,12},{12,14},{14,16},{16,18},{18... | collective-permute-start | bytes 24584 | tf_op jit(solution)/shard_map/ppermute | solution.py:19
where the time goes:
time: 124 us; the launch traced here: 122 us
  local copies, waits for them, and re-layouts  30.6 us (25%)
  starting transfers between devices  29.1 us (23%)
  other arithmetic  22 us (18%)
  matrix products  21.2 us (17%)
  between operations  12.9 us (10%)
  waiting for transfers between devices  5.49 us (4%)
    unnamed x80, local copies, waits for them, and re-layouts  20.5 us
    eq x16, other arithmetic, lookup(): low_hot = (low_part[None] == levels[:, None, None]).astype(jnp.bfloat16)  12.6 us
    all_to_all x2, starting transfers between devices, body(): lax.all_to_all(pieces.astype(jnp.bfloat16), 'depth', split_axis=0, concat...  12.3 us
    dot_general x16, matrix products, lookup(): jnp.einsum('chl,lgk->chgk', table, low_hot, preferred_element_type=jnp.fl...  10.1 us
    dot_general x8, matrix products, shear_columns(): jnp.einsum('crbk,kj->bjcr', windows, tap_matrix, preferred_element_type=j...  8.45 us
    ppermute x3, starting transfers between devices, extended(): before = lax.ppermute(last, axis, up)  8.45 us
    ppermute x3, starting transfers between devices, extended(): after = lax.ppermute(first, axis, down)  8.41 us
    ppermute x3, waiting for transfers between devices, extended(): before = lax.ppermute(last, axis, up)  4.03 us
  transfers between devices with their start and end apart: 8, of which 2 were waited for; matrix products, arithmetic and copies ran while one was open for 21% of the time, Pallas kernels for 0%

commit v1 on v0

v1 whole, which is shorter than its diff:
```python
import functools

import jax
import jax.numpy as jnp
from jax import lax
from jax.experimental import pallas as pl
from jax.experimental.pallas import tpu as pltpu

VIEWS = 2
MARGIN = 16
PAD = 128
LANES = 128
MESH = pl.DeviceIdType.MESH


def lanczos(t):
    def sinc(u):
        x = jnp.float32(jnp.pi) * u
        safe = jnp.where(u == 0.0, 1.0, x)
        return jnp.where(u == 0.0, 1.0, jnp.sin(safe) / safe)

    return jnp.where(jnp.abs(t) < 3.0, sinc(t) * sinc(t / 3.0), 0.0)


def take(table_row, index):
    table = jnp.broadcast_to(table_row, index.shape)
    return jnp.take_along_axis(table, index, axis=1, mode="promise_in_bounds")


def replicate_alpha(part, lane):
    width = LANES // 4
    alpha = jnp.where(lane >= 3 * width, part, 0.0)
    alpha = alpha + pltpu.roll(alpha, 2 * width, 1)
    return alpha + pltpu.roll(alpha, width, 1)


def kernel(
    sizes, code_ref, volume_ref, tf_ref, out_ref,
    edge_ref, halo_ref, cls_ref, wx_ref, wy_ref, sheared_ref, picture_ref,
    s1_ref, r1_ref, s2_ref, r2_ref, k2_ref, s3_ref, r3_ref, own_ref, fin_ref,
    halo_send, halo_recv, send1, recv1, send2, recv2, send3, recv3, send4, recv4,
):
    depth_size, band_size = sizes
    slabs, rows, extent = volume_ref.shape
    wide = rows + 2 * MARGIN
    stations = depth_size // 4
    chunk = extent // stations
    strip = chunk // 4
    window = chunk + 2 * PAD
    total_depth = slabs * depth_size
    slots = 1 if band_size == 2 else 2
    d = lax.axis_index("depth")
    band = lax.axis_index("band")
    core = lax.rem(d, 2)
    col = lax.rem(lax.div(d, 2), 2)
    z = lax.div(d, 4)
    peer1 = d + 1 - 2 * core
    peer2 = d + 2 - 4 * col
    offsets = [(k + 1) // 2 if k % 2 else stations - k // 2 for k in range(1, stations)]
    offsets = sorted(offsets, key=lambda k: -min(k, stations - k)) + [0]

    def at_depth(i):
        return (i, band)

    barrier = pltpu.get_barrier_semaphore()

    def greet(device):
        pl.semaphore_signal(barrier, inc=1, device_id=device, device_id_type=MESH)

    @pl.when(band > 0)
    def _():
        greet((d, band - 1))

    @pl.when(band < band_size - 1)
    def _():
        greet((d, band + 1))

    greet(at_depth(peer1))
    greet(at_depth(peer2))
    for k in offsets[:-1]:
        greet(at_depth(lax.rem(z + k, stations) * 4 + lax.rem(d, 4)))

    @pl.when(d > 0)
    def _():
        greet(at_depth(d - 1))

    @pl.when(d < depth_size - 1)
    def _():
        greet(at_depth(d + 1))

    for s in range(slabs):
        edge_ref[0, s] = volume_ref[s, rows - MARGIN : rows, :].astype(jnp.float32).astype(jnp.bfloat16)
        edge_ref[1, s] = volume_ref[s, 0:MARGIN, :].astype(jnp.float32).astype(jnp.bfloat16)

    def neighbours(i, n):
        return lax.div(i + n - 1, n) + 1 - lax.div(i + 1, n)

    pl.semaphore_wait(
        barrier, 1 + len(offsets) + neighbours(d, depth_size) + neighbours(band, band_size))

    def to_next():
        return pltpu.make_async_remote_copy(
            edge_ref.at[0], halo_ref.at[0], halo_send.at[0], halo_recv.at[0],
            device_id=(d, lax.rem(band + 1, band_size)), device_id_type=MESH)

    def to_previous():
        last = slots - 1
        return pltpu.make_async_remote_copy(
            edge_ref.at[1], halo_ref.at[last], halo_send.at[1], halo_recv.at[last],
            device_id=(d, lax.rem(band + band_size - 1, band_size)), device_id_type=MESH)

    @pl.when(band < band_size - 1)
    def _():
        to_next().start()

    @pl.when(band > 0)
    def _():
        to_previous().start()

    table = tf_ref[...].astype(jnp.float32)
    opacity = table[3:4] / (64.0 * total_depth)
    palette = jnp.concatenate([table[0:3] / 255.0 * opacity, opacity], axis=0)
    palette = palette.astype(jnp.bfloat16).astype(jnp.float32)

    def classify(s, codes, row, lane0):
        low = codes & (LANES - 1)
        upper = codes >= LANES
        for c in range(4):
            first = take(palette[c : c + 1, 0:LANES], low)
            second = take(palette[c : c + 1, LANES : 2 * LANES], low)
            cls_ref[s, c * wide + row : c * wide + row + 16, PAD + lane0 : PAD + lane0 + LANES] = (
                jnp.where(upper, second, first).astype(jnp.bfloat16))

    def own_rows(s, carry):
        zeros = jnp.zeros((4 * wide, PAD), jnp.bfloat16)
        cls_ref[s, :, 0:PAD] = zeros
        cls_ref[s, :, PAD + extent : 2 * PAD + extent] = zeros
        for r in range(0, rows, 16):
            for x in range(0, extent, LANES):
                classify(s, volume_ref[s, r : r + 16, x : x + LANES], r, x)
        return carry

    lax.fori_loop(0, slabs, own_rows, 0)

    count = VIEWS * slabs
    row_id = lax.broadcasted_iota(jnp.int32, (2 * count, LANES), 0)
    whole = jnp.zeros((2 * count, LANES), jnp.float32)
    frac = jnp.zeros((2 * count, LANES), jnp.float32)
    period = 2 * total_depth
    for axis in range(2):
        for v in range(VIEWS):
            for s in range(slabs):
                position = d * slabs + s
                num = code_ref[v, axis] * (2 * position + 1 - total_depth)
                w = lax.div(num + 64 * period, period) - 64
                f = (num - w * period).astype(jnp.float32) / float(period)
                here = row_id == axis * count + v * slabs + s
                whole = jnp.where(here, w.astype(jnp.float32), whole)
                frac = jnp.where(here, f, frac)
    lane_f = lax.broadcasted_iota(jnp.int32, (2 * count, LANES), 1).astype(jnp.float32)
    taps = lanczos(frac - (lane_f - float(LANES // 2) - whole))

    lane16 = lax.broadcasted_iota(jnp.int32, (16, LANES), 1)
    row16 = lax.broadcasted_iota(jnp.int32, (16, LANES), 0)
    diagonal = (lane16 - row16) & (LANES - 1)
    zero_tile = jnp.zeros((16, LANES), jnp.bfloat16)
    pieces = window // LANES
    for v in range(VIEWS):
        for s in range(slabs):
            base = take(taps[v * slabs + s : v * slabs + s + 1], diagonal)
            turned = {}
            for i in range(chunk // 16):
                start = 16 * i + LANES // 2
                first, turn = start // LANES, start % LANES
                if turn not in turned:
                    moved = pltpu.roll(base, turn, 1) if turn else base
                    turned[turn] = (
                        jnp.where(lane16 >= turn, moved, 0.0).astype(jnp.bfloat16),
                        jnp.where(lane16 < turn, moved, 0.0).astype(jnp.bfloat16))
                row = v * chunk + 16 * i
                for m in range(pieces):
                    tile = turned[turn][0] if m == first else turned[turn][1] if m == first + 1 else zero_tile
                    wx_ref[s, row : row + 16, m * LANES : (m + 1) * LANES] = tile

    group = lane16 // rows
    y = lane16 - group * rows
    for v in range(VIEWS):
        for s in range(slabs):
            at = count + v * slabs + s
            for r in range(0, wide, 16):
                if r < rows:
                    position = r
                elif slots == 1 and r == rows:
                    position = jnp.where(band == 0, rows, -MARGIN)
                else:
                    position = -MARGIN if r == rows else rows
                unused = slots == 1 and r > rows
                index = row16 + position - y + LANES // 2
                tile = jnp.zeros((16, LANES), jnp.float32) if unused else take(taps[at : at + 1], index)
                for c in range(4):
                    k = c * wide + r
                    wy_ref[v * slabs + s, k : k + 16, 0:LANES] = jnp.where(group == c, tile, 0.0).astype(jnp.bfloat16)
                    wy_ref[v * slabs + s, k : k + 16, LANES : 2 * LANES] = tile.astype(jnp.bfloat16) if c == 3 else zero_tile

    @pl.when(d == 0)
    def _():
        fin_ref[:, 0:MARGIN, :] = jnp.zeros((VIEWS, MARGIN, LANES), jnp.float32)

    @pl.when(d == depth_size - 1)
    def _():
        fin_ref[:, MARGIN + strip : 2 * MARGIN + strip, :] = jnp.zeros((VIEWS, MARGIN, LANES), jnp.float32)

    has = [band > 0, band < band_size - 1] if slots == 2 else [None]
    if slots == 1:
        @pl.when(band == 0)
        def _():
            to_next().wait()

        @pl.when(band > 0)
        def _():
            to_previous().wait()
    else:
        @pl.when(band < band_size - 1)
        def _():
            to_next().wait_send()
            to_previous().wait_recv()

        @pl.when(band > 0)
        def _():
            to_previous().wait_send()
            to_next().wait_recv()

    def far_rows(s, carry):
        for slot in range(2):
            row = rows + slot * MARGIN

            def fill():
                for c in range(4):
                    cls_ref[s, c * wide + row : c * wide + row + 16, PAD : PAD + extent] = jnp.zeros((16, extent), jnp.bfloat16)

            def look():
                for x in range(0, extent, LANES):
                    codes = halo_ref[slot, s, :, x : x + LANES].astype(jnp.float32).astype(jnp.int32)
                    classify(s, codes, row, x)

            if slot >= slots:
                fill()
            elif slots == 1:
                look()
            else:
                pl.when(has[slot])(look)
                pl.when(jnp.logical_not(has[slot]))(fill)
        return carry

    lax.fori_loop(0, slabs, far_rows, 0)

    facing = [code_ref[v, 3] >= 0 for v in range(VIEWS)]
    lane_s = lax.broadcasted_iota(jnp.int32, (strip, LANES), 1)

    def over(ahead, near, far):
        front = jnp.where(ahead, near, far)
        back = jnp.where(ahead, far, near)
        return front + (1.0 - replicate_alpha(front, lane_s)) * back

    def station(step):
        return lax.rem(z + offsets[step], stations)

    def first_copy(step):
        return pltpu.make_async_remote_copy(
            s1_ref.at[step], r1_ref.at[step], send1.at[step], recv1.at[step],
            device_id=at_depth(peer1), device_id_type=MESH)

    def second_copy(step):
        return pltpu.make_async_remote_copy(
            s2_ref.at[step], r2_ref.at[step], send2.at[step], recv2.at[step],
            device_id=at_depth(peer2), device_id_type=MESH)

    def third_copy(step):
        return pltpu.make_async_remote_copy(
            s3_ref.at[step], r3_ref.at[z], send3.at[step], recv3.at[step],
            device_id=at_depth(station(step) * 4 + lax.rem(d, 4)), device_id_type=MESH)

    def render(step):
        start = pl.multiple_of(station(step) * chunk, LANES)

        def shear(s, carry):
            data = cls_ref[s, :, pl.ds(start, window)]
            moved = lax.dot_general(
                wx_ref[s], data, (((1,), (1,)), ((), ())), preferred_element_type=jnp.float32
            ).astype(jnp.bfloat16)
            for v in range(VIEWS):
                sheared_ref[v, s] = jnp.dot(
                    moved[v * chunk : (v + 1) * chunk], wy_ref[v * slabs + s],
                    preferred_element_type=jnp.float32)
            return carry

        lax.fori_loop(0, slabs, shear, 0)
        for v in range(VIEWS):
            for q in range(4):
                part = slice(q * strip, (q + 1) * strip)
                picture = None
                for k in range(slabs):
                    at = jnp.where(facing[v], slabs - 1 - k, k)
                    color = sheared_ref[v, at, part, 0:LANES]
                    if picture is None:
                        picture = color
                    else:
                        picture = color + (1.0 - sheared_ref[v, at, part, LANES : 2 * LANES]) * picture
                picture_ref[step, v, q] = picture
            for h in range(2):
                s1_ref[step, v, h] = picture_ref[step, v, 2 * h + 1 - core].astype(jnp.bfloat16)
        first_copy(step).start()

    def merge1(step):
        first_copy(step).wait()
        for v in range(VIEWS):
            ahead = (core == 0) == facing[v]
            for h, keep in ((1 - col, False), (col, True)):
                near = picture_ref[step, v, 2 * h + core]
                both = over(ahead, near, r1_ref[step, v, h].astype(jnp.float32))
                if keep:
                    k2_ref[step, v] = both
                else:
                    s2_ref[step, v] = both.astype(jnp.bfloat16)
        second_copy(step).start()

    def merge2(step):
        second_copy(step).wait()
        for v in range(VIEWS):
            ahead = (col == 0) == facing[v]
            both = over(ahead, k2_ref[step, v], r2_ref[step, v].astype(jnp.float32))
            if step == stations - 1:
                own_ref[v] = both
            else:
                s3_ref[step, v] = both.astype(jnp.bfloat16)
        if step < stations - 1:
            third_copy(step).start()

    r3_ref[z] = jnp.zeros((VIEWS, strip, LANES), jnp.bfloat16)
    for step in range(stations + 2):
        if step < stations:
            render(step)
        if 0 <= step - 1 < stations:
            merge1(step - 1)
        if 0 <= step - 2 < stations:
            merge2(step - 2)

    taps_in = strip + 2 * MARGIN
    column = lax.broadcasted_iota(jnp.int32, (strip, taps_in), 0)
    source = lax.broadcasted_iota(jnp.int32, (strip, taps_in), 1)
    double = float(2 * extent)
    weights = []
    for v in range(VIEWS):
        num = (code_ref[v, 2] * (2 * (d * strip + column) + 1 - extent) + extent).astype(jnp.float32)
        whole_w = jnp.floor(num / double)
        frac_w = (num - whole_w * double) / double
        weights.append(lanczos(frac_w - ((source - MARGIN - column).astype(jnp.float32) - whole_w)))

    for step in range(stations - 1):
        third_copy(step).wait()

    for v in range(VIEWS):
        picture = None
        for k in range(stations):
            at = jnp.where(facing[v], stations - 1 - k, k)
            part = jnp.where(at == z, own_ref[v], r3_ref[at, v].astype(jnp.float32))
            if picture is None:
                picture = part
            else:
                picture = part + (1.0 - replicate_alpha(part, lane_s)) * picture
        fin_ref[v, MARGIN : MARGIN + strip] = picture

    def to_left():
        return pltpu.make_async_remote_copy(
            fin_ref.at[:, MARGIN : 2 * MARGIN], fin_ref.at[:, MARGIN + strip : 2 * MARGIN + strip],
            send4.at[0], recv4.at[0],
            device_id=at_depth(lax.rem(d + depth_size - 1, depth_size)), device_id_type=MESH)

    def to_right():
        return pltpu.make_async_remote_copy(
            fin_ref.at[:, strip : MARGIN + strip], fin_ref.at[:, 0:MARGIN],
            send4.at[1], recv4.at[1],
            device_id=at_depth(lax.rem(d + 1, depth_size)), device_id_type=MESH)

    @pl.when(d > 0)
    def _():
        to_left().start()

    @pl.when(d < depth_size - 1)
    def _():
        to_right().start()

    @pl.when(d > 0)
    def _():
        to_left().wait_send()
        to_right().wait_recv()

    @pl.when(d < depth_size - 1)
    def _():
        to_right().wait_send()
        to_left().wait_recv()

    for v in range(VIEWS):
        out_ref[v] = jnp.dot(
            weights[v], fin_ref[v], precision=lax.Precision.HIGHEST, preferred_element_type=jnp.float32)


def body(volume, tf_table, view_code):
    depth_size, band_size = lax.axis_size("depth"), lax.axis_size("band")
    slabs, rows, extent = volume.shape
    wide = rows + 2 * MARGIN
    stations = depth_size // 4
    chunk = extent // stations
    strip = chunk // 4
    slots = 1 if band_size == 2 else 2
    bf16, f32 = jnp.bfloat16, jnp.float32
    vmem = pl.BlockSpec(memory_space=pltpu.VMEM)
    dma = pltpu.SemaphoreType.DMA
    out = pl.pallas_call(
        functools.partial(kernel, (depth_size, band_size)),
        out_shape=jax.ShapeDtypeStruct((VIEWS, strip, LANES), f32),
        in_specs=[pl.BlockSpec(memory_space=pltpu.SMEM), vmem, vmem],
        out_specs=vmem,
        scratch_shapes=[
            pltpu.VMEM((2, slabs, MARGIN, extent), bf16),
            pltpu.VMEM((slots, slabs, MARGIN, extent), bf16),
            pltpu.VMEM((slabs, 4 * wide, extent + 2 * PAD), bf16),
            pltpu.VMEM((slabs, VIEWS * chunk, chunk + 2 * PAD), bf16),
            pltpu.VMEM((VIEWS * slabs, 4 * wide, 2 * LANES), bf16),
            pltpu.VMEM((VIEWS, slabs, chunk, 2 * LANES), f32),
            pltpu.VMEM((stations, VIEWS, 4, strip, LANES), f32),
            pltpu.VMEM((stations, VIEWS, 2, strip, LANES), bf16),
            pltpu.VMEM((stations, VIEWS, 2, strip, LANES), bf16),
            pltpu.VMEM((stations, VIEWS, strip, LANES), bf16),
            pltpu.VMEM((stations, VIEWS, strip, LANES), bf16),
            pltpu.VMEM((stations, VIEWS, strip, LANES), f32),
            pltpu.VMEM((stations, VIEWS, strip, LANES), bf16),
            pltpu.VMEM((stations, VIEWS, strip, LANES), bf16),
            pltpu.VMEM((VIEWS, strip, LANES), f32),
            pltpu.VMEM((VIEWS, strip + 2 * MARGIN, LANES), f32),
            dma((2,)), dma((slots,)),
            dma((stations,)), dma((stations,)),
            dma((stations,)), dma((stations,)),
            dma((stations,)), dma((stations,)),
            dma((2,)), dma((2,)),
        ],
        compiler_params=pltpu.CompilerParams(collective_id=0, has_side_effects=True),
    )(view_code, volume, tf_table)
    return out.reshape(VIEWS, strip, 4, rows)


def solution(mesh):
    P = jax.sharding.PartitionSpec
    placed = (P("depth", "band", None), P(), P())
    return jax.shard_map(
        body, mesh=mesh, in_specs=placed, out_specs=P(None, "depth", None, "band"), check_vma=False
    )
```

time: 124 us -> 32.9 us (0.27)
  the two profiles are of different devices: /device:TPU:8 before, /device:TPU:1 now
where the time goes in v1:
time: 32.9 us; the launch traced here: 32.7 us
  Pallas kernels  31.1 us (95%)
  local copies, waits for them, and re-layouts  1.6 us (5%)
    pallas_call x1, Pallas kernels, body(): pl.pallas_call(functools.partial(kernel, (depth_size, band_size)), out_sh...  31.1 us
    pallas_call x1, local copies, waits for them, and re-layouts, body(): pl.pallas_call(functools.partial(kernel, (depth_size, band_size)), out_sh...  1.6 us

profile of v1, /device:TPU:1, one launch (start us, length us, event | category | flops | bytes accessed | tf_op | source)
XLA Modules:
  0.0 32.7 jit_solution(8019559008302764342)
XLA Ops:
  0.0 31.1 %shard_map.37 = f32[2,64,128]{2,1,0:T(8,128)} custom-call(s32[2,4]{1,0:T(2,128)} %code_ref.1, s32[4,32,1024]{2,1,0:T(8,128)} %volume_ref.1, s32[4,256]{1,0:T(4,128)} %tf_ref.1), custom_call_target="tpu_custom_call" | custom-call | tf_op jit(solution)/shard_map/pallas_call | solution.py:419
  31.1 1.6 %copy.5 = f32[2,64,128]{1,2,0:T(8,128)} copy(f32[2,64,128]{2,1,0:T(8,128)} %shard_map.37) | data formatting | bytes 131072 | tf_op jit(solution)/shard_map/pallas_call | solution.py:419

commit v2 on v1

--- a/solution.py
+++ b/solution.py
@@ -37,8 +37,8 @@
 def kernel(
     sizes, code_ref, volume_ref, tf_ref, out_ref,
     edge_ref, halo_ref, cls_ref, wx_ref, wy_ref, sheared_ref, picture_ref,
-    s1_ref, r1_ref, s2_ref, r2_ref, k2_ref, s3_ref, r3_ref, own_ref, fin_ref,
-    halo_send, halo_recv, send1, recv1, send2, recv2, send3, recv3, send4, recv4,
+    s1_ref, r1_ref, s2_ref, r2_ref, k2_ref, s3_ref, r3_ref, own_ref,
+    halo_send, halo_recv, send1, recv1, send2, recv2, send3, recv3,
 ):
     depth_size, band_size = sizes
     slabs, rows, extent = volume_ref.shape
@@ -47,6 +47,8 @@
     chunk = extent // stations
     strip = chunk // 4
     window = chunk + 2 * PAD
+    reach = chunk + 2 * MARGIN
+    piece = strip + 2 * MARGIN
     total_depth = slabs * depth_size
     slots = 1 if band_size == 2 else 2
     d = lax.axis_index("depth")
@@ -80,14 +82,6 @@
     for k in offsets[:-1]:
         greet(at_depth(lax.rem(z + k, stations) * 4 + lax.rem(d, 4)))
 
-    @pl.when(d > 0)
-    def _():
-        greet(at_depth(d - 1))
-
-    @pl.when(d < depth_size - 1)
-    def _():
-        greet(at_depth(d + 1))
-
     for s in range(slabs):
         edge_ref[0, s] = volume_ref[s, rows - MARGIN : rows, :].astype(jnp.float32).astype(jnp.bfloat16)
         edge_ref[1, s] = volume_ref[s, 0:MARGIN, :].astype(jnp.float32).astype(jnp.bfloat16)
@@ -96,7 +90,7 @@
         return lax.div(i + n - 1, n) + 1 - lax.div(i + 1, n)
 
     pl.semaphore_wait(
-        barrier, 1 + len(offsets) + neighbours(d, depth_size) + neighbours(band, band_size))
+        barrier, 1 + len(offsets) + neighbours(band, band_size))
 
     def to_next():
         return pltpu.make_async_remote_copy(
@@ -169,15 +163,15 @@
         for s in range(slabs):
             base = take(taps[v * slabs + s : v * slabs + s + 1], diagonal)
             turned = {}
-            for i in range(chunk // 16):
-                start = 16 * i + LANES // 2
+            for i in range(reach // 16):
+                start = 16 * i - MARGIN + LANES // 2
                 first, turn = start // LANES, start % LANES
                 if turn not in turned:
                     moved = pltpu.roll(base, turn, 1) if turn else base
                     turned[turn] = (
                         jnp.where(lane16 >= turn, moved, 0.0).astype(jnp.bfloat16),
                         jnp.where(lane16 < turn, moved, 0.0).astype(jnp.bfloat16))
-                row = v * chunk + 16 * i
+                row = v * reach + 16 * i
                 for m in range(pieces):
                     tile = turned[turn][0] if m == first else turned[turn][1] if m == first + 1 else zero_tile
                     wx_ref[s, row : row + 16, m * LANES : (m + 1) * LANES] = tile
@@ -202,14 +196,6 @@
                     wy_ref[v * slabs + s, k : k + 16, 0:LANES] = jnp.where(group == c, tile, 0.0).astype(jnp.bfloat16)
                     wy_ref[v * slabs + s, k : k + 16, LANES : 2 * LANES] = tile.astype(jnp.bfloat16) if c == 3 else zero_tile
 
-    @pl.when(d == 0)
-    def _():
-        fin_ref[:, 0:MARGIN, :] = jnp.zeros((VIEWS, MARGIN, LANES), jnp.float32)
-
-    @pl.when(d == depth_size - 1)
-    def _():
-        fin_ref[:, MARGIN + strip : 2 * MARGIN + strip, :] = jnp.zeros((VIEWS, MARGIN, LANES), jnp.float32)
-
     has = [band > 0, band < band_size - 1] if slots == 2 else [None]
     if slots == 1:
         @pl.when(band == 0)
@@ -255,7 +241,7 @@
     lax.fori_loop(0, slabs, far_rows, 0)
 
     facing = [code_ref[v, 3] >= 0 for v in range(VIEWS)]
-    lane_s = lax.broadcasted_iota(jnp.int32, (strip, LANES), 1)
+    lane_s = lax.broadcasted_iota(jnp.int32, (piece, LANES), 1)
 
     def over(ahead, near, far):
         front = jnp.where(ahead, near, far)
@@ -279,6 +265,9 @@
         return pltpu.make_async_remote_copy(
             s3_ref.at[step], r3_ref.at[z], send3.at[step], recv3.at[step],
             device_id=at_depth(station(step) * 4 + lax.rem(d, 4)), device_id_type=MESH)
+
+    def strip_of(step, v, q):
+        return picture_ref[step, v, pl.ds(pl.multiple_of(q * strip, 16), piece), :]
 
     def render(step):
         start = pl.multiple_of(station(step) * chunk, LANES)
@@ -290,14 +279,14 @@
             ).astype(jnp.bfloat16)
             for v in range(VIEWS):
                 sheared_ref[v, s] = jnp.dot(
-                    moved[v * chunk : (v + 1) * chunk], wy_ref[v * slabs + s],
+                    moved[v * reach : (v + 1) * reach], wy_ref[v * slabs + s],
                     preferred_element_type=jnp.float32)
             return carry
 
-        lax.fori_loop(0, slabs, shear, 0)
+        lax.fori_loop(0, slabs, shear, 0, unroll=True)
         for v in range(VIEWS):
-            for q in range(4):
-                part = slice(q * strip, (q + 1) * strip)
+            for q in range(0, reach, 32):
+                part = slice(q, q + 32)
                 picture = None
                 for k in range(slabs):
                     at = jnp.where(facing[v], slabs - 1 - k, k)
@@ -306,9 +295,9 @@
                         picture = color
                     else:
                         picture = color + (1.0 - sheared_ref[v, at, part, LANES : 2 * LANES]) * picture
-                picture_ref[step, v, q] = picture
+                picture_ref[step, v, part] = picture
             for h in range(2):
-                s1_ref[step, v, h] = picture_ref[step, v, 2 * h + 1 - core].astype(jnp.bfloat16)
+                s1_ref[step, v, h] = strip_of(step, v, 2 * h + 1 - core).astype(jnp.bfloat16)
         first_copy(step).start()
 
     def merge1(step):
@@ -316,7 +305,7 @@
         for v in range(VIEWS):
             ahead = (core == 0) == facing[v]
             for h, keep in ((1 - col, False), (col, True)):
-                near = picture_ref[step, v, 2 * h + core]
+                near = strip_of(step, v, 2 * h + core)
                 both = over(ahead, near, r1_ref[step, v, h].astype(jnp.float32))
                 if keep:
                     k2_ref[step, v] = both
@@ -336,7 +325,7 @@
         if step < stations - 1:
             third_copy(step).start()
 
-    r3_ref[z] = jnp.zeros((VIEWS, strip, LANES), jnp.bfloat16)
+    r3_ref[z] = jnp.zeros((VIEWS, piece, LANES), jnp.bfloat16)
     for step in range(stations + 2):
         if step < stations:
             render(step)
@@ -345,16 +334,19 @@
         if 0 <= step - 2 < stations:
             merge2(step - 2)
 
-    taps_in = strip + 2 * MARGIN
+    taps_in = piece
     column = lax.broadcasted_iota(jnp.int32, (strip, taps_in), 0)
     source = lax.broadcasted_iota(jnp.int32, (strip, taps_in), 1)
     double = float(2 * extent)
+    column_in = d * strip + source - MARGIN
+    inside = jnp.logical_and(column_in >= 0, column_in < extent)
     weights = []
     for v in range(VIEWS):
         num = (code_ref[v, 2] * (2 * (d * strip + column) + 1 - extent) + extent).astype(jnp.float32)
         whole_w = jnp.floor(num / double)
         frac_w = (num - whole_w * double) / double
-        weights.append(lanczos(frac_w - ((source - MARGIN - column).astype(jnp.float32) - whole_w)))
+        tap = lanczos(frac_w - ((source - MARGIN - column).astype(jnp.float32) - whole_w))
+        weights.append(jnp.where(inside, tap, 0.0))
 
     for step in range(stations - 1):
         third_copy(step).wait()
@@ -368,41 +360,9 @@
                 picture = part
             else:
                 picture = part + (1.0 - replicate_alpha(part, lane_s)) * picture
-        fin_ref[v, MARGIN : MARGIN + strip] = picture
-
-    def to_left():
-        return pltpu.make_async_remote_copy(
-            fin_ref.at[:, MARGIN : 2 * MARGIN], fin_ref.at[:, MARGIN + strip : 2 * MARGIN + strip],
-            send4.at[0], recv4.at[0],
-            device_id=at_depth(lax.rem(d + depth_size - 1, depth_size)), device_id_type=MESH)
-
-    def to_right():
-        return pltpu.make_async_remote_copy(
-            fin_ref.at[:, strip : MARGIN + strip], fin_ref.at[:, 0:MARGIN],
-            send4.at[1], recv4.at[1],
-            device_id=at_depth(lax.rem(d + 1, depth_size)), device_id_type=MESH)
-
-    @pl.when(d > 0)
-    def _():
-        to_left().start()
-
-    @pl.when(d < depth_size - 1)
-    def _():
-        to_right().start()
-
-    @pl.when(d > 0)
-    def _():
-        to_left().wait_send()
-        to_right().wait_recv()
-
-    @pl.when(d < depth_size - 1)
-    def _():
-        to_right().wait_send()
-        to_left().wait_recv()
-
-    for v in range(VIEWS):
-        out_ref[v] = jnp.dot(
-            weights[v], fin_ref[v], precision=lax.Precision.HIGHEST, preferred_element_type=jnp.float32)
+        final = jnp.dot(
+            weights[v], picture, precision=lax.Precision.HIGHEST, preferred_element_type=jnp.float32)
+        out_ref[v] = final.T
 
 
 def body(volume, tf_table, view_code):
@@ -412,41 +372,41 @@
     stations = depth_size // 4
     chunk = extent // stations
     strip = chunk // 4
+    reach = chunk + 2 * MARGIN
+    piece = strip + 2 * MARGIN
     slots = 1 if band_size == 2 else 2
     bf16, f32 = jnp.bfloat16, jnp.float32
     vmem = pl.BlockSpec(memory_space=pltpu.VMEM)
     dma = pltpu.SemaphoreType.DMA
     out = pl.pallas_call(
         functools.partial(kernel, (depth_size, band_size)),
-        out_shape=jax.ShapeDtypeStruct((VIEWS, strip, LANES), f32),
+        out_shape=jax.ShapeDtypeStruct((VIEWS, LANES, strip), f32),
         in_specs=[pl.BlockSpec(memory_space=pltpu.SMEM), vmem, vmem],
         out_specs=vmem,
         scratch_shapes=[
             pltpu.VMEM((2, slabs, MARGIN, extent), bf16),
             pltpu.VMEM((slots, slabs, MARGIN, extent), bf16),
             pltpu.VMEM((slabs, 4 * wide, extent + 2 * PAD), bf16),
-            pltpu.VMEM((slabs, VIEWS * chunk, chunk + 2 * PAD), bf16),
+            pltpu.VMEM((slabs, VIEWS * reach, chunk + 2 * PAD), bf16),
             pltpu.VMEM((VIEWS * slabs, 4 * wide, 2 * LANES), bf16),
-            pltpu.VMEM((VIEWS, slabs, chunk, 2 * LANES), f32),
-            pltpu.VMEM((stations, VIEWS, 4, strip, LANES), f32),
-            pltpu.VMEM((stations, VIEWS, 2, strip, LANES), bf16),
-            pltpu.VMEM((stations, VIEWS, 2, strip, LANES), bf16),
-            pltpu.VMEM((stations, VIEWS, strip, LANES), bf16),
-            pltpu.VMEM((stations, VIEWS, strip, LANES), bf16),
-            pltpu.VMEM((stations, VIEWS, strip, LANES), f32),
-            pltpu.VMEM((stations, VIEWS, strip, LANES), bf16),
-            pltpu.VMEM((stations, VIEWS, strip, LANES), bf16),
-            pltpu.VMEM((VIEWS, strip, LANES), f32),
-            pltpu.VMEM((VIEWS, strip + 2 * MARGIN, LANES), f32),
+            pltpu.VMEM((VIEWS, slabs, reach, 2 * LANES), f32),
+            pltpu.VMEM((stations, VIEWS, reach, LANES), f32),
+            pltpu.VMEM((stations, VIEWS, 2, piece, LANES), bf16),
+            pltpu.VMEM((stations, VIEWS, 2, piece, LANES), bf16),
+            pltpu.VMEM((stations, VIEWS, piece, LANES), bf16),
+            pltpu.VMEM((stations, VIEWS, piece, LANES), bf16),
+            pltpu.VMEM((stations, VIEWS, piece, LANES), f32),
+            pltpu.VMEM((stations, VIEWS, piece, LANES), bf16),
+            pltpu.VMEM((stations, VIEWS, piece, LANES), bf16),
+            pltpu.VMEM((VIEWS, piece, LANES), f32),
             dma((2,)), dma((slots,)),
             dma((stations,)), dma((stations,)),
             dma((stations,)), dma((stations,)),
             dma((stations,)), dma((stations,)),
-            dma((2,)), dma((2,)),
         ],
         compiler_params=pltpu.CompilerParams(collective_id=0, has_side_effects=True),
     )(view_code, volume, tf_table)
-    return out.reshape(VIEWS, strip, 4, rows)
+    return out.reshape(VIEWS, 4, rows, strip).transpose(0, 3, 1, 2)
 
 
 def solution(mesh):

time: 32.9 us -> 30.7 us (0.933)
  the two profiles are of different devices: /device:TPU:1 before, /device:TPU:0 now
where the time goes in v2:
time: 30.7 us; the launch traced here: 30.5 us
  Pallas kernels  29 us (94%)
  local copies, waits for them, and re-layouts  1.57 us (5%)
    pallas_call x1, Pallas kernels, body(): pl.pallas_call(functools.partial(kernel, (depth_size, band_size)), out_sh...  29 us
    unnamed x1, local copies, waits for them, and re-layouts  1.57 us

profile of v2, /device:TPU:0, one launch (start us, length us, event | category | flops | bytes accessed | tf_op | source)
XLA Modules:
  0.0 30.5 jit_solution(563869208183562279)
XLA Ops:
  0.0 29.0 %shard_map.37 = f32[2,128,64]{2,1,0:T(8,128)} custom-call(s32[2,4]{1,0:T(2,128)} %code_ref.1, s32[4,32,1024]{2,1,0:T(8,128)} %volume_ref.1, s32[4,256]{1,0:T(4,128)} %tf_ref.1), custom_call_target="tpu_custom_call" | custom-call | tf_op jit(solution)/shard_map/pallas_call | solution.py:381
  29.0 1.6 %copy.5 = f32[2,64,4,32]{1,3,2,0:T(8,128)} copy(f32[2,64,4,32]{1,3,2,0:T(8,128)} %bitcast.3) | data formatting | bytes 131072

commit v3 on v2

--- a/solution.py
+++ b/solution.py
@@ -58,8 +58,19 @@
     z = lax.div(d, 4)
     peer1 = d + 1 - 2 * core
     peer2 = d + 2 - 4 * col
-    offsets = [(k + 1) // 2 if k % 2 else stations - k // 2 for k in range(1, stations)]
-    offsets = sorted(offsets, key=lambda k: -min(k, stations - k)) + [0]
+    half = stations // 2
+    low = 1 - lax.div(z, half)
+
+    def mirrored(i):
+        return i * low + (stations - 1 - i) * (1 - low)
+
+    def station(step):
+        if step < half:
+            return mirrored(stations - 1 - step)
+        if step == stations - 1:
+            return z
+        u, inner = step - half, half - 1 - mirrored(z)
+        return mirrored(jnp.where(u < inner, half - 1 - u, u - inner))
 
     def at_depth(i):
         return (i, band)
@@ -79,7 +90,7 @@
 
     greet(at_depth(peer1))
     greet(at_depth(peer2))
-    for k in offsets[:-1]:
+    for k in range(1, stations):
         greet(at_depth(lax.rem(z + k, stations) * 4 + lax.rem(d, 4)))
 
     for s in range(slabs):
@@ -90,26 +101,40 @@
         return lax.div(i + n - 1, n) + 1 - lax.div(i + 1, n)
 
     pl.semaphore_wait(
-        barrier, 1 + len(offsets) + neighbours(band, band_size))
-
-    def to_next():
+        barrier, 1 + stations + neighbours(band, band_size))
+
+    units, near_units = extent // LANES, chunk // LANES + 1
+    cuts = ((units - near_units, units), (units // 2 - 1, units - near_units), (0, units // 2 - 1))
+
+    def lanes_of(g):
+        first, last = cuts[g]
+        start = first * low + (units - last) * (1 - low)
+        return pl.multiple_of(start * LANES, LANES), last - first
+
+    def group_of(ref, slot, g):
+        start, width = lanes_of(g)
+        return ref.at[slot, :, :, pl.ds(start, width * LANES)]
+
+    def to_next(g):
         return pltpu.make_async_remote_copy(
-            edge_ref.at[0], halo_ref.at[0], halo_send.at[0], halo_recv.at[0],
+            group_of(edge_ref, 0, g), group_of(halo_ref, 0, g), halo_send.at[0, g], halo_recv.at[0, g],
             device_id=(d, lax.rem(band + 1, band_size)), device_id_type=MESH)
 
-    def to_previous():
+    def to_previous(g):
         last = slots - 1
         return pltpu.make_async_remote_copy(
-            edge_ref.at[1], halo_ref.at[last], halo_send.at[1], halo_recv.at[last],
+            group_of(edge_ref, 1, g), group_of(halo_ref, last, g), halo_send.at[1, g], halo_recv.at[last, g],
             device_id=(d, lax.rem(band + band_size - 1, band_size)), device_id_type=MESH)
 
     @pl.when(band < band_size - 1)
     def _():
-        to_next().start()
+        for g in range(3):
+            to_next(g).start()
 
     @pl.when(band > 0)
     def _():
-        to_previous().start()
+        for g in range(3):
+            to_previous(g).start()
 
     table = tf_ref[...].astype(jnp.float32)
     opacity = table[3:4] / (64.0 * total_depth)
@@ -122,7 +147,7 @@
         for c in range(4):
             first = take(palette[c : c + 1, 0:LANES], low)
             second = take(palette[c : c + 1, LANES : 2 * LANES], low)
-            cls_ref[s, c * wide + row : c * wide + row + 16, PAD + lane0 : PAD + lane0 + LANES] = (
+            cls_ref[s, c * wide + row : c * wide + row + 16, pl.ds(PAD + lane0, LANES)] = (
                 jnp.where(upper, second, first).astype(jnp.bfloat16))
 
     def own_rows(s, carry):
@@ -197,48 +222,52 @@
                     wy_ref[v * slabs + s, k : k + 16, LANES : 2 * LANES] = tile.astype(jnp.bfloat16) if c == 3 else zero_tile
 
     has = [band > 0, band < band_size - 1] if slots == 2 else [None]
-    if slots == 1:
-        @pl.when(band == 0)
-        def _():
-            to_next().wait()
-
-        @pl.when(band > 0)
-        def _():
-            to_previous().wait()
-    else:
-        @pl.when(band < band_size - 1)
-        def _():
-            to_next().wait_send()
-            to_previous().wait_recv()
-
-        @pl.when(band > 0)
-        def _():
-            to_previous().wait_send()
-            to_next().wait_recv()
-
-    def far_rows(s, carry):
-        for slot in range(2):
-            row = rows + slot * MARGIN
-
-            def fill():
-                for c in range(4):
-                    cls_ref[s, c * wide + row : c * wide + row + 16, PAD : PAD + extent] = jnp.zeros((16, extent), jnp.bfloat16)
-
-            def look():
-                for x in range(0, extent, LANES):
-                    codes = halo_ref[slot, s, :, x : x + LANES].astype(jnp.float32).astype(jnp.int32)
-                    classify(s, codes, row, x)
-
-            if slot >= slots:
-                fill()
-            elif slots == 1:
-                look()
+    def clear(slot):
+        row = rows + slot * MARGIN
+        for s in range(slabs):
+            for c in range(4):
+                cls_ref[s, c * wide + row : c * wide + row + 16, PAD : PAD + extent] = jnp.zeros((16, extent), jnp.bfloat16)
+
+    for slot in range(2):
+        if slot >= slots:
+            clear(slot)
+        elif slots == 2:
+            pl.when(jnp.logical_not(has[slot]))(functools.partial(clear, slot))
+
+    def far_rows(g):
+        if slots == 1:
+            @pl.when(band == 0)
+            def _():
+                to_next(g).wait()
+
+            @pl.when(band > 0)
+            def _():
+                to_previous(g).wait()
+        else:
+            @pl.when(band < band_size - 1)
+            def _():
+                to_next(g).wait_send()
+                to_previous(g).wait_recv()
+
+            @pl.when(band > 0)
+            def _():
+                to_previous(g).wait_send()
+                to_next(g).wait_recv()
+
+        start, width = lanes_of(g)
+
+        def look(slot):
+            for s in range(slabs):
+                for i in range(width):
+                    x = pl.multiple_of(start + i * LANES, LANES)
+                    codes = halo_ref[slot, s, :, pl.ds(x, LANES)].astype(jnp.float32).astype(jnp.int32)
+                    classify(s, codes, rows + slot * MARGIN, x)
+
+        for slot in range(slots):
+            if slots == 1:
+                look(slot)
             else:
-                pl.when(has[slot])(look)
-                pl.when(jnp.logical_not(has[slot]))(fill)
-        return carry
-
-    lax.fori_loop(0, slabs, far_rows, 0)
+                pl.when(has[slot])(functools.partial(look, slot))
 
     facing = [code_ref[v, 3] >= 0 for v in range(VIEWS)]
     lane_s = lax.broadcasted_iota(jnp.int32, (piece, LANES), 1)
@@ -248,9 +277,6 @@
         back = jnp.where(ahead, far, near)
         return front + (1.0 - replicate_alpha(front, lane_s)) * back
 
-    def station(step):
-        return lax.rem(z + offsets[step], stations)
-
     def first_copy(step):
         return pltpu.make_async_remote_copy(
             s1_ref.at[step], r1_ref.at[step], send1.at[step], recv1.at[step],
@@ -263,7 +289,7 @@
 
     def third_copy(step):
         return pltpu.make_async_remote_copy(
-            s3_ref.at[step], r3_ref.at[z], send3.at[step], recv3.at[step],
+            s3_ref.at[step], r3_ref.at[z], send3.at[step], recv3.at[z],
             device_id=at_depth(station(step) * 4 + lax.rem(d, 4)), device_id_type=MESH)
 
     def strip_of(step, v, q):
@@ -283,7 +309,10 @@
                     preferred_element_type=jnp.float32)
             return carry
 
-        lax.fori_loop(0, slabs, shear, 0, unroll=True)
+        for s in range(slabs):
+            shear(s, 0)
+            if s == slabs // 2 - 1 and step > 0:
+                merge1(step - 1)
         for v in range(VIEWS):
             for q in range(0, reach, 32):
                 part = slice(q, q + 32)
@@ -328,8 +357,10 @@
     r3_ref[z] = jnp.zeros((VIEWS, piece, LANES), jnp.bfloat16)
     for step in range(stations + 2):
         if step < stations:
+            if step in (0, 1, half):
+                far_rows((0, 1, half).index(step))
             render(step)
-        if 0 <= step - 1 < stations:
+        if step == stations:
             merge1(step - 1)
         if 0 <= step - 2 < stations:
             merge2(step - 2)
@@ -349,7 +380,12 @@
         weights.append(jnp.where(inside, tap, 0.0))
 
     for step in range(stations - 1):
-        third_copy(step).wait()
+        third_copy(step).wait_send()
+    for k in range(1, stations):
+        other = lax.rem(z + k, stations)
+        pltpu.make_async_remote_copy(
+            s3_ref.at[0], r3_ref.at[other], send3.at[0], recv3.at[other],
+            device_id=at_depth(other * 4 + lax.rem(d, 4)), device_id_type=MESH).wait_recv()
 
     for v in range(VIEWS):
         picture = None
@@ -399,7 +435,7 @@
             pltpu.VMEM((stations, VIEWS, piece, LANES), bf16),
             pltpu.VMEM((stations, VIEWS, piece, LANES), bf16),
             pltpu.VMEM((VIEWS, piece, LANES), f32),
-            dma((2,)), dma((slots,)),
+            dma((2, 3)), dma((slots, 3)),
             dma((stations,)), dma((stations,)),
             dma((stations,)), dma((stations,)),
             dma((stations,)), dma((stations,)),

time: 30.7 us -> 29.4 us (0.958)
  Pallas kernels: 29 us -> 27.6 us
    pallas_call x1, Pallas kernels: 29 us -> 27.6 us  [body(): pl.pallas_call(functools.partial(kernel, (depth_size, band_size)), out_sh...]
where the time goes in v3:
time: 29.4 us; the launch traced here: 29.2 us
  Pallas kernels  27.6 us (94%)
  local copies, waits for them, and re-layouts  1.57 us (5%)
    pallas_call x1, Pallas kernels, body(): pl.pallas_call(functools.partial(kernel, (depth_size, band_size)), out_sh...  27.6 us
    unnamed x1, local copies, waits for them, and re-layouts  1.57 us

profile of v3, /device:TPU:0, one launch (start us, length us, event | category | flops | bytes accessed | tf_op | source)
XLA Modules:
  0.0 29.2 jit_solution(491757369495096325)
XLA Ops:
  0.0 27.6 %shard_map.37 = f32[2,128,64]{2,1,0:T(8,128)} custom-call(s32[2,4]{1,0:T(2,128)} %code_ref.1, s32[4,32,1024]{2,1,0:T(8,128)} %volume_ref.1, s32[4,256]{1,0:T(4,128)} %tf_ref.1), custom_call_target="tpu_custom_call" | custom-call | tf_op jit(solution)/shard_map/pallas_call | solution.py:417
  27.6 1.6 %copy.5 = f32[2,64,4,32]{1,3,2,0:T(8,128)} copy(f32[2,64,4,32]{1,3,2,0:T(8,128)} %bitcast.3) | data formatting | bytes 131072
